TPU v7x, 512 devices: a whole 4x8x8 slice. The times are simulated.
512 devices in a mesh: row: 16 (over z, core), col: 32 (over x, y).
Axes of the slice: x: 4, y: 8, z: 8, core: 2. Of those that a mesh axis runs over, the one named last changes fastest.
Arguments:
- graph_emb: float32 [16384, 256], P('row', 'col'), may hold values from -40 to 40
- conf_emb: float32 [16384, 256], P('col', 'row'), may hold values from -40 to 40
Outputs:
- grad_graph: float32 [16384, 256], P('row', 'col')
- grad_conf: float32 [16384, 256], P('col', 'row')
- row_potential: float32 [16384], P('row')
- col_potential: float32 [16384], P('col')
All inputs are finite; a program needn't handle non-finite values.
Results may differ from a plain program's by a relative error of at most 0.0003.
Values sent between devices are 32-bit elements; how exact they have to be, the bound alone decides.
No kernel may reach another device: no remote copies, remote signals or barrier semaphores. Data moves between devices by JAX's collectives and lax.ppermute only.
A program may use at most 64 MiB of HBM per device.

v0:
```python
import math
import jax
import jax.numpy as jnp
from jax import lax
from jax.sharding import PartitionSpec as P

ITERS = 3
entropy_weight = 1.0


def across_columns(scores):
    local_max = jnp.max(scores, axis=1)
    peak_value = lax.pmax(local_max, "col")
    exp_total = lax.psum(jnp.sum(jnp.exp(scores - peak_value[:, None]), axis=1), "col")
    return peak_value + jnp.log(exp_total)


def across_rows(scores):
    local_max = jnp.max(scores, axis=0)
    peak_value = lax.pmax(local_max, "row")
    exp_total = lax.psum(jnp.sum(jnp.exp(scores - peak_value[None, :]), axis=0), "row")
    return peak_value + jnp.log(exp_total)


def per_device(graph_emb, conf_emb):
    graph_block = lax.all_gather(graph_emb, "col", axis=1, tiled=True)
    conf_block = lax.all_gather(conf_emb, "row", axis=1, tiled=True)
    batch_size = graph_block.shape[0] * lax.axis_size("row")
    feature_scale = graph_block.shape[1] ** (-0.5)
    cost_tile = (
        -lax.dot_general(
            graph_block,
            conf_block,
            (((1,), (1,)), ((), ())),
            precision=lax.Precision.HIGHEST,
            preferred_element_type=jnp.float32,
        )
        * feature_scale
    )
    log_weight = -math.log(batch_size)
    row_pot = jnp.zeros((graph_block.shape[0],), jnp.float32)
    col_pot = jnp.zeros((conf_block.shape[0],), jnp.float32)
    for sweep_index in range(ITERS):
        row_pot = entropy_weight * (
            log_weight - across_columns((col_pot[None, :] - cost_tile) / entropy_weight)
        )
        col_pot = entropy_weight * (
            log_weight - across_rows((row_pot[:, None] - cost_tile) / entropy_weight)
        )
    transport = jnp.exp((row_pot[:, None] + col_pot[None, :] - cost_tile) / entropy_weight)
    factor = -batch_size * feature_scale
    graph_term = (
        jnp.dot(
            transport,
            conf_block,
            precision=lax.Precision.HIGHEST,
            preferred_element_type=jnp.float32,
        )
        * factor
    )
    conf_term = (
        lax.dot_general(
            transport,
            graph_block,
            (((0,), (0,)), ((), ())),
            precision=lax.Precision.HIGHEST,
            preferred_element_type=jnp.float32,
        )
        * factor
    )
    graph_total = lax.psum(graph_term, "col")
    conf_total = lax.psum(conf_term, "row")
    graph_width = graph_term.shape[1] // lax.axis_size("col")
    conf_width = conf_term.shape[1] // lax.axis_size("row")
    grad_graph = lax.dynamic_slice_in_dim(
        graph_total, lax.axis_index("col") * graph_width, graph_width, 1
    )
    grad_conf = lax.dynamic_slice_in_dim(
        conf_total, lax.axis_index("row") * conf_width, conf_width, 1
    )
    return (grad_graph, grad_conf, row_pot, col_pot)


def solution(mesh):
    return jax.shard_map(
        per_device,
        mesh=mesh,
        in_specs=(P("row", "col"), P("col", "row")),
        out_specs=(P("row", "col"), P("col", "row"), P("row"), P("col")),
        check_vma=False,
    )
```

profile of v0, /device:TPU:64, one launch (start us, length us, event | category | flops | bytes accessed | tf_op | source)
XLA Modules:
  0.0 959.0 jit_solution(13728568763963591692)
XLA Ops:
  7.2 0.0 all-gather.2.cloned.1.call-start
  7.2 0.7 all-gather.2.cloned.1.call-update
  7.9 0.0 all-reduce.5.cloned.1.call-start
  7.9 21.8 %all_gather.7 = f32[512,256]{0,1:T(8,128)S(1)} all-gather(f32[512,16]{0,1:T(8,128)} %param.3), channel_id=1, replica_groups=mesh['row'=16,'col'=32] {'row'}, dimensions={1}, use_global_device_ids=true | all-gather | bytes 557056 | tf_op jit(solution)/shard_map/all_gather | solution.py:27
  29.7 67.0 %all-gather.2.cloned.1.call-done = f32[1024,256]{0,1:T(8,128)} async-done(((f32[1024,8]{0,1:T(8,128)}), f32[1024,256]{0,1:T(8,128)}) %all-gather.2.cloned.1.call-update) | async-done | bytes 1048592 | tf_op jit(solution)/shard_map/all_gather | solution.py:26
  96.7 3.2 subtract_reduce_fusion.5
  99.9 72.0 %pmax.42 = f32[1024]{0:T(1024)S(1)} all-reduce(f32[1024]{0:T(1024)S(1)} %get-tuple-element.4), channel_id=1, replica_groups=mesh['row'=16,'col'=32] {'col'}, use_global_device_ids=true, to_apply=%region_1.0 | all-reduce | flops 1024 | bytes 8192 | tf_op jit(solution)/shard_map/pmax | solution.py:13
  172.0 0.5 exponential_reduce_fusion.5
  172.5 69.6 %psum.56 = f32[1024]{0:T(1024)S(1)} all-reduce(f32[1024]{0:T(1024)S(1)} %exponential_reduce_fusion.5), channel_id=1, replica_groups=mesh['row'=16,'col'=32] {'col'}, use_global_device_ids=true, to_apply=%region_3.0 | all-reduce | flops 1024 | bytes 8192 | tf_op jit(solution)/shard_map/psum | solution.py:14
  242.2 0.2 subtract_reduce_fusion.4
  242.4 21.1 %pmax.43 = f32[512]{0:T(512)S(1)} all-reduce(f32[512]{0:T(512)S(1)} %subtract_reduce_fusion.4), channel_id=1, replica_groups=mesh['row'=16,'col'=32] {'row'}, use_global_device_ids=true, to_apply=%region_5.0 | all-reduce | flops 512 | bytes 4096 | tf_op jit(solution)/shard_map/pmax | solution.py:20
  263.5 0.4 exponential_reduce_fusion.4
  263.9 23.9 %psum.57 = f32[512]{0:T(512)S(1)} all-reduce(f32[512]{0:T(512)S(1)} %exponential_reduce_fusion.4), channel_id=1, replica_groups=mesh['row'=16,'col'=32] {'row'}, use_global_device_ids=true, to_apply=%region_7.0 | all-reduce | flops 512 | bytes 4096 | tf_op jit(solution)/shard_map/psum | solution.py:21
  287.8 0.2 subtract_reduce_fusion.3
  288.0 71.7 %pmax.44 = f32[1024]{0:T(1024)S(1)} all-reduce(f32[1024]{0:T(1024)S(1)} %subtract_reduce_fusion.3), channel_id=1, replica_groups=mesh['row'=16,'col'=32] {'col'}, use_global_device_ids=true, to_apply=%region_9.0 | all-reduce | flops 1024 | bytes 8192 | tf_op jit(solution)/shard_map/pmax | solution.py:13
  359.7 0.6 exponential_reduce_fusion.3
  360.3 69.6 %psum.58 = f32[1024]{0:T(1024)S(1)} all-reduce(f32[1024]{0:T(1024)S(1)} %exponential_reduce_fusion.3), channel_id=1, replica_groups=mesh['row'=16,'col'=32] {'col'}, use_global_device_ids=true, to_apply=%region_11.0 | all-reduce | flops 1024 | bytes 8192 | tf_op jit(solution)/shard_map/psum | solution.py:14
  429.9 0.2 subtract_reduce_fusion.2
  430.1 23.5 %pmax.45 = f32[512]{0:T(512)S(1)} all-reduce(f32[512]{0:T(512)S(1)} %subtract_reduce_fusion.2), channel_id=1, replica_groups=mesh['row'=16,'col'=32] {'row'}, use_global_device_ids=true, to_apply=%region_13.0 | all-reduce | flops 512 | bytes 4096 | tf_op jit(solution)/shard_map/pmax | solution.py:20
  453.7 0.4 exponential_reduce_fusion.2
  454.1 23.5 %psum.59 = f32[512]{0:T(512)S(1)} all-reduce(f32[512]{0:T(512)S(1)} %exponential_reduce_fusion.2), channel_id=1, replica_groups=mesh['row'=16,'col'=32] {'row'}, use_global_device_ids=true, to_apply=%region_15.0 | all-reduce | flops 512 | bytes 4096 | tf_op jit(solution)/shard_map/psum | solution.py:21
  477.7 0.2 subtract_reduce_fusion.1
  477.9 71.6 %pmax.46 = f32[1024]{0:T(1024)S(1)} all-reduce(f32[1024]{0:T(1024)S(1)} %subtract_reduce_fusion.1), channel_id=1, replica_groups=mesh['row'=16,'col'=32] {'col'}, use_global_device_ids=true, to_apply=%region_17.0 | all-reduce | flops 1024 | bytes 8192 | tf_op jit(solution)/shard_map/pmax | solution.py:13
  549.5 0.6 exponential_reduce_fusion.1
  550.1 69.6 %psum.60 = f32[1024]{0:T(1024)S(1)} all-reduce(f32[1024]{0:T(1024)S(1)} %exponential_reduce_fusion.1), channel_id=1, replica_groups=mesh['row'=16,'col'=32] {'col'}, use_global_device_ids=true, to_apply=%region_19.0 | all-reduce | flops 1024 | bytes 8192 | tf_op jit(solution)/shard_map/psum | solution.py:14
  619.8 0.0 copy-start
  619.8 0.2 subtract_reduce_fusion
  620.0 23.5 %pmax.47 = f32[512]{0:T(512)S(1)} all-reduce(f32[512]{0:T(512)S(1)} %subtract_reduce_fusion), channel_id=1, replica_groups=mesh['row'=16,'col'=32] {'row'}, use_global_device_ids=true, to_apply=%region_21.0 | all-reduce | flops 512 | bytes 4096 | tf_op jit(solution)/shard_map/pmax | solution.py:20
  643.5 0.4 exponential_reduce_fusion
  644.0 23.5 %psum.61 = f32[512]{0:T(512)S(1)} all-reduce(f32[512]{0:T(512)S(1)} %exponential_reduce_fusion), channel_id=1, replica_groups=mesh['row'=16,'col'=32] {'row'}, use_global_device_ids=true, to_apply=%region_23.0 | all-reduce | flops 512 | bytes 4096 | tf_op jit(solution)/shard_map/psum | solution.py:21
  667.5 0.0 copy-start.1
  667.5 4.4 fusion.3
  671.9 0.0 all-reduce.5.cloned.1.call-update
  672.0 0.2 all-reduce.3.cloned.1.call-start
  672.2 0.0 copy-done
  672.2 0.0 copy-done.1
  672.2 3.4 fusion.2
  675.6 0.0 all-reduce.3.cloned.1.call-update
  675.6 108.3 %all-reduce.5.cloned.1.call-done = f32[512,256]{0,1:T(8,128)} async-done(((f32[512,256]{0,1:T(8,128)}), f32[512,256]{0,1:T(8,128)}) %all-reduce.5.cloned.1.call-update) | async-done | bytes 524304 | tf_op jit(solution)/shard_map/psum | solution.py:72
  783.9 1.4 constant_dynamic-slice_fusion
  785.3 165.8 %all-reduce.3.cloned.1.call-done = f32[1024,256]{0,1:T(8,128)} async-done(((f32[1024,256]{0,1:T(8,128)}), f32[1024,256]{0,1:T(8,128)}) %all-reduce.3.cloned.1.call-update) | async-done | bytes 1048592 | tf_op jit(solution)/shard_map/psum | solution.py:71
  951.1 1.4 constant_dynamic-slice_fusion.1
  (6 shorter events, 0.1 us)
Async XLA Ops:
  7.2 89.5 %all-gather.2.cloned.1.call-start = ((), (), s32[]{:S(2)}) async-start(), calls=%async_computation | async-start | bytes 1081344 | tf_op jit(solution)/shard_map/all_gather | solution.py:26
  7.9 776.0 %all-reduce.5.cloned.1.call-start = ((), (), s32[]{:S(2)}) async-start(), calls=%async_computation.2 | async-start | bytes 1048576 | tf_op jit(solution)/shard_map/psum | solution.py:72
  619.8 52.4 %copy-start = (f32[1024]{0:T(1024)}, f32[1024]{0:T(1024)S(1)}, u32[]{:S(2)}) copy-start(f32[1024]{0:T(1024)S(1)} %add_subtract_fusion) | copy-start | bytes 12292
  667.5 4.7 copy-start.1
  672.0 279.2 %all-reduce.3.cloned.1.call-start = ((), (), s32[]{:S(2)}) async-start(), calls=%async_computation.1 | async-start | bytes 2097152 | tf_op jit(solution)/shard_map/psum | solution.py:71
Sparse Core Ops, SparseCore 0:
  11.1 85.4 all-gather.1
  672.1 111.8 all-reduce.4
  787.4 163.6 all-reduce.2
where the time goes:
time: 960 us; the launch traced here: 959 us
  blocking collectives  585 us (61%)
  waiting for transfers between devices  342 us (36%)
  between operations  13.8 us (1%)
  matrix products  11 us (1%)
    pmax x3, blocking collectives, across_columns(): peak_value = lax.pmax(local_max, 'col')  215 us
    psum x3, blocking collectives, across_columns(): lax.psum(jnp.sum(jnp.exp(scores - peak_value[:, None]), axis=1), 'col')  209 us
    psum x1, waiting for transfers between devices, per_device(): graph_total = lax.psum(graph_term, 'col')  166 us
    psum x1, waiting for transfers between devices, per_device(): conf_total = lax.psum(conf_term, 'row')  108 us
    psum x3, blocking collectives, across_rows(): lax.psum(jnp.sum(jnp.exp(scores - peak_value[None, :]), axis=0), 'row')  71 us
    pmax x3, blocking collectives, across_rows(): peak_value = lax.pmax(local_max, 'row')  68.2 us
    all_gather x1, waiting for transfers between devices, per_device(): graph_block = lax.all_gather(graph_emb, 'col', axis=1, tiled=True)  67 us
    all_gather x1, blocking collectives, per_device(): conf_block = lax.all_gather(conf_emb, 'row', axis=1, tiled=True)  21.8 us
  transfers between devices with their start and end apart: 3, of which 3 were waited for; matrix products, arithmetic and copies ran while one was open for 0% of the time, Pallas kernels for 0%

commit v1 on v0

--- a/solution.py
+++ b/solution.py
@@ -23,7 +23,8 @@
 
 
 def per_device(graph_emb, conf_emb):
-    graph_block = lax.all_gather(graph_emb, "col", axis=1, tiled=True)
+    sent = jnp.stack([graph_emb] * lax.axis_size("col"))
+    graph_block = jnp.concatenate(lax.all_to_all(sent, "col", 0, 0), axis=1)
     conf_block = lax.all_gather(conf_emb, "row", axis=1, tiled=True)
     batch_size = graph_block.shape[0] * lax.axis_size("row")
     feature_scale = graph_block.shape[1] ** (-0.5)

time: 960 us -> 913 us (0.951)
  waiting for transfers between devices: 342 us -> 279 us
  starting transfers between devices: 0.3 us -> 10.3 us
    all_gather x1 -> x0, waiting for transfers between devices: 67 us -> none  [per_device(): graph_block = lax.all_gather(graph_emb, 'col', axis=1, tiled=True)]
    all_to_all x0 -> x1, starting transfers between devices: none -> 10.1 us  [per_device(): graph_block = jnp.concatenate(lax.all_to_all(sent, 'col', 0, 0), axis=1)]
  transfers between devices with their start and end apart: 3 -> 3, of which waited for: 3 -> 3; matrix products, arithmetic and copies ran while one was open for 0% -> 1% of each run, Pallas kernels for 0% -> 0%
where the time goes in v1:
time: 913 us; the launch traced here: 912 us
  blocking collectives  589 us (65%)
  waiting for transfers between devices  279 us (31%)
  between operations  14.1 us (2%)
  matrix products  11 us (1%)
  starting transfers between devices  10.3 us (1%)
    pmax x3, blocking collectives, across_columns(): peak_value = lax.pmax(local_max, 'col')  215 us
    psum x3, blocking collectives, across_columns(): lax.psum(jnp.sum(jnp.exp(scores - peak_value[:, None]), axis=1), 'col')  209 us
    psum x1, waiting for transfers between devices, per_device(): graph_total = lax.psum(graph_term, 'col')  166 us
    psum x1, waiting for transfers between devices, per_device(): conf_total = lax.psum(conf_term, 'row')  106 us
    pmax x3, blocking collectives, across_rows(): peak_value = lax.pmax(local_max, 'row')  72.5 us
    psum x3, blocking collectives, across_rows(): lax.psum(jnp.sum(jnp.exp(scores - peak_value[None, :]), axis=0), 'row')  71 us
    all_gather x1, blocking collectives, per_device(): conf_block = lax.all_gather(conf_emb, 'row', axis=1, tiled=True)  21.6 us
  transfers between devices with their start and end apart: 3, of which 3 were waited for; matrix products, arithmetic and copies ran while one was open for 1% of the time, Pallas kernels for 0%

profile of v1, /device:TPU:64, one launch (start us, length us, event | category | flops | bytes accessed | tf_op | source)
XLA Modules:
  0.0 912.5 jit_solution(6976317515702388879)
XLA Ops:
  7.2 0.0 copy-start.1
  7.2 1.9 stack.2
  9.1 10.1 %all-to-all-start = ((f32[32,1024,8]{1,2,0:T(8,128)}), f32[32,1024,8]{1,2,0:T(8,128)}, u32[]{:S(2)}, u32[]{:S(2)}) async-start(f32[32,1024,8]{1,2,0:T(8,128)} %stack.2), calls=%async_computation | async-start | bytes 2097152 | tf_op jit(solution)/shard_map/all_to_all | solution.py:27
  19.2 0.0 all-reduce.5.cloned.1.call-start
  19.2 0.0 copy-done.1
  19.2 21.6 %all_gather.3 = f32[512,256]{0,1:T(8,128)S(1)} all-gather(f32[512,16]{0,1:T(8,128)S(1)} %copy-done.1), channel_id=1, replica_groups=mesh['row'=16,'col'=32] {'row'}, dimensions={1}, use_global_device_ids=true | all-gather | bytes 557056 | tf_op jit(solution)/shard_map/all_gather | solution.py:28
  40.8 7.0 all-to-all-done
  47.8 3.2 subtract_reduce_fusion.5
  51.0 72.0 %pmax.42 = f32[1024]{0:T(1024)S(1)} all-reduce(f32[1024]{0:T(1024)S(1)} %get-tuple-element.4), channel_id=1, replica_groups=mesh['row'=16,'col'=32] {'col'}, use_global_device_ids=true, to_apply=%region_1.0 | all-reduce | flops 1024 | bytes 8192 | tf_op jit(solution)/shard_map/pmax | solution.py:13
  123.0 0.5 exponential_reduce_fusion.5
  123.5 69.6 %psum.56 = f32[1024]{0:T(1024)S(1)} all-reduce(f32[1024]{0:T(1024)S(1)} %exponential_reduce_fusion.5), channel_id=1, replica_groups=mesh['row'=16,'col'=32] {'col'}, use_global_device_ids=true, to_apply=%region_3.0 | all-reduce | flops 1024 | bytes 8192 | tf_op jit(solution)/shard_map/psum | solution.py:14
  193.2 0.2 subtract_reduce_fusion.4
  193.4 25.4 %pmax.43 = f32[512]{0:T(512)S(1)} all-reduce(f32[512]{0:T(512)S(1)} %subtract_reduce_fusion.4), channel_id=1, replica_groups=mesh['row'=16,'col'=32] {'row'}, use_global_device_ids=true, to_apply=%region_5.0 | all-reduce | flops 512 | bytes 4096 | tf_op jit(solution)/shard_map/pmax | solution.py:20
  218.8 0.4 exponential_reduce_fusion.4
  219.3 23.9 %psum.57 = f32[512]{0:T(512)S(1)} all-reduce(f32[512]{0:T(512)S(1)} %exponential_reduce_fusion.4), channel_id=1, replica_groups=mesh['row'=16,'col'=32] {'row'}, use_global_device_ids=true, to_apply=%region_7.0 | all-reduce | flops 512 | bytes 4096 | tf_op jit(solution)/shard_map/psum | solution.py:21
  243.2 0.2 subtract_reduce_fusion.3
  243.4 71.7 %pmax.44 = f32[1024]{0:T(1024)S(1)} all-reduce(f32[1024]{0:T(1024)S(1)} %subtract_reduce_fusion.3), channel_id=1, replica_groups=mesh['row'=16,'col'=32] {'col'}, use_global_device_ids=true, to_apply=%region_9.0 | all-reduce | flops 1024 | bytes 8192 | tf_op jit(solution)/shard_map/pmax | solution.py:13
  315.1 0.6 exponential_reduce_fusion.3
  315.6 69.6 %psum.58 = f32[1024]{0:T(1024)S(1)} all-reduce(f32[1024]{0:T(1024)S(1)} %exponential_reduce_fusion.3), channel_id=1, replica_groups=mesh['row'=16,'col'=32] {'col'}, use_global_device_ids=true, to_apply=%region_11.0 | all-reduce | flops 1024 | bytes 8192 | tf_op jit(solution)/shard_map/psum | solution.py:14
  385.3 0.2 subtract_reduce_fusion.2
  385.5 23.5 %pmax.45 = f32[512]{0:T(512)S(1)} all-reduce(f32[512]{0:T(512)S(1)} %subtract_reduce_fusion.2), channel_id=1, replica_groups=mesh['row'=16,'col'=32] {'row'}, use_global_device_ids=true, to_apply=%region_13.0 | all-reduce | flops 512 | bytes 4096 | tf_op jit(solution)/shard_map/pmax | solution.py:20
  409.0 0.4 exponential_reduce_fusion.2
  409.5 23.5 %psum.59 = f32[512]{0:T(512)S(1)} all-reduce(f32[512]{0:T(512)S(1)} %exponential_reduce_fusion.2), channel_id=1, replica_groups=mesh['row'=16,'col'=32] {'row'}, use_global_device_ids=true, to_apply=%region_15.0 | all-reduce | flops 512 | bytes 4096 | tf_op jit(solution)/shard_map/psum | solution.py:21
  433.0 0.2 subtract_reduce_fusion.1
  433.3 71.6 %pmax.46 = f32[1024]{0:T(1024)S(1)} all-reduce(f32[1024]{0:T(1024)S(1)} %subtract_reduce_fusion.1), channel_id=1, replica_groups=mesh['row'=16,'col'=32] {'col'}, use_global_device_ids=true, to_apply=%region_17.0 | all-reduce | flops 1024 | bytes 8192 | tf_op jit(solution)/shard_map/pmax | solution.py:13
  504.9 0.6 exponential_reduce_fusion.1
  505.4 69.6 %psum.60 = f32[1024]{0:T(1024)S(1)} all-reduce(f32[1024]{0:T(1024)S(1)} %exponential_reduce_fusion.1), channel_id=1, replica_groups=mesh['row'=16,'col'=32] {'col'}, use_global_device_ids=true, to_apply=%region_19.0 | all-reduce | flops 1024 | bytes 8192 | tf_op jit(solution)/shard_map/psum | solution.py:14
  575.1 0.0 copy-start
  575.1 0.2 subtract_reduce_fusion
  575.3 23.5 %pmax.47 = f32[512]{0:T(512)S(1)} all-reduce(f32[512]{0:T(512)S(1)} %subtract_reduce_fusion), channel_id=1, replica_groups=mesh['row'=16,'col'=32] {'row'}, use_global_device_ids=true, to_apply=%region_21.0 | all-reduce | flops 512 | bytes 4096 | tf_op jit(solution)/shard_map/pmax | solution.py:20
  598.9 0.4 exponential_reduce_fusion
  599.3 23.5 %psum.61 = f32[512]{0:T(512)S(1)} all-reduce(f32[512]{0:T(512)S(1)} %exponential_reduce_fusion), channel_id=1, replica_groups=mesh['row'=16,'col'=32] {'row'}, use_global_device_ids=true, to_apply=%region_23.0 | all-reduce | flops 512 | bytes 4096 | tf_op jit(solution)/shard_map/psum | solution.py:21
  622.9 0.0 copy-start.2
  622.9 4.4 fusion.3
  627.3 0.0 all-reduce.5.cloned.1.call-update
  627.3 0.2 all-reduce.3.cloned.1.call-start
  627.5 0.0 copy-done
  627.5 0.0 copy-done.2
  627.6 3.4 fusion.2
  630.9 0.0 all-reduce.3.cloned.1.call-update
  630.9 106.2 %all-reduce.5.cloned.1.call-done = f32[512,256]{0,1:T(8,128)} async-done(((f32[512,256]{0,1:T(8,128)}), f32[512,256]{0,1:T(8,128)}) %all-reduce.5.cloned.1.call-update) | async-done | bytes 524304 | tf_op jit(solution)/shard_map/psum | solution.py:73
  737.1 1.4 constant_dynamic-slice_fusion
  738.5 165.8 %all-reduce.3.cloned.1.call-done = f32[1024,256]{0,1:T(8,128)} async-done(((f32[1024,256]{0,1:T(8,128)}), f32[1024,256]{0,1:T(8,128)}) %all-reduce.3.cloned.1.call-update) | async-done | bytes 1048592 | tf_op jit(solution)/shard_map/psum | solution.py:72
  904.3 1.4 constant_dynamic-slice_fusion.1
  (6 shorter events, 0.1 us)
Async XLA Ops:
  7.2 12.1 %copy-start.1 = (f32[512,16]{0,1:T(8,128)S(1)}, f32[512,16]{0,1:T(8,128)}, u32[]{:S(2)}) copy-start(f32[512,16]{0,1:T(8,128)} %param.3) | copy-start | bytes 98308
  9.1 38.7 %all-to-all-start = ((f32[32,1024,8]{1,2,0:T(8,128)}), f32[32,1024,8]{1,2,0:T(8,128)}, u32[]{:S(2)}, u32[]{:S(2)}) async-start(f32[32,1024,8]{1,2,0:T(8,128)} %stack.2), calls=%async_computation | async-start | bytes 2097152 | tf_op jit(solution)/shard_map/all_to_all | solution.py:27
  19.2 717.9 %all-reduce.5.cloned.1.call-start = ((), (), s32[]{:S(2)}) async-start(), calls=%async_computation.2 | async-start | bytes 1048576 | tf_op jit(solution)/shard_map/psum | solution.py:73
  575.1 52.4 %copy-start = (f32[1024]{0:T(1024)}, f32[1024]{0:T(1024)S(1)}, u32[]{:S(2)}) copy-start(f32[1024]{0:T(1024)S(1)} %add_subtract_fusion) | copy-start | bytes 12292
  622.9 4.7 copy-start.2
  627.3 277.0 %all-reduce.3.cloned.1.call-start = ((), (), s32[]{:S(2)}) async-start(), calls=%async_computation.1 | async-start | bytes 2097152 | tf_op jit(solution)/shard_map/psum | solution.py:72
Sparse Core Ops, SparseCore 0:
  627.4 109.6 all-reduce.4
  740.5 163.6 all-reduce.2
